TPU v7x, 256 devices: a whole 4x4x8 slice. The times are simulated.
256 devices in a mesh: inst: 8 (over x, y_lo), space: 32 (over z, y_hi, core).
Axes of the slice: x: 4, y: 4 (y_hi: 2, y_lo: 2; y = y_hi * 2 + y_lo), z: 8, core: 2. Of those that a mesh axis runs over, the one named last changes fastest.
Arguments:
- adjoint: float32 [8, 5, 256, 64, 128], P('inst', None, 'space'), may hold values from -6 to 6
- source: float32 [8, 5, 256, 64, 128], P('inst', None, 'space'), may hold values from -6 to 6
- viscosity: float32 [256, 64, 128], P('space'), may hold values from 0.2 to 2
- kappa: float32 [5], replicated, may hold values from 0.5 to 2
- coupling: float32 [5, 5], replicated, may hold values from -2.4 to 2.4
- bc_flags: int32 [5, 3], replicated, may hold values 0 or 1
- inst_map: int32 [8], replicated, may hold values from 0 to 7, each once
Outputs:
- residual: float32 [8, 5, 256, 64, 128], P('inst', None, 'space')
Inputs may be any that keep to these rules, and one draw needn't show every extreme that they name: `inst_map`: a permutation of 0 to 7. `bc_flags`: 1 marks a face of zero normal flux, 0 a face held at zero.
All inputs are finite; a program needn't handle non-finite values.
Results may differ from a plain program's by a relative error of at most 0.0001.
Values sent between devices are 32-bit elements; how exact they have to be, the bound alone decides.
A program may use at most 128 MiB of HBM per device.

v0:
```python
import jax
import jax.numpy as jnp
from jax import lax
from jax.sharding import PartitionSpec as P


def with_halo(block, sides, width):
    for axis, dim in sides:
        count = lax.axis_size(axis)
        forward = [(i, i + 1) for i in range(count - 1)]
        forward.append((count - 1, 0))
        backward = [(target, source) for source, target in forward]
        low = lax.ppermute(
            lax.slice_in_dim(block, block.shape[dim] - width, None, axis=dim), axis, forward
        )
        high = lax.ppermute(lax.slice_in_dim(block, 0, width, axis=dim), axis, backward)
        block = jnp.concatenate([low, block, high], axis=dim)
    return block


def spectral_matrix(labels, slots):
    offset = labels[:, None] - labels[None, :]
    parity = (1 - 2 * (jnp.abs(offset) % 2)).astype(jnp.float32)
    sines = jnp.sin(jnp.pi * offset.astype(jnp.float32) / slots)
    safe = jnp.where(offset == 0, jnp.float32(1.0), sines)
    return jnp.where(offset == 0, jnp.float32(0.0), 0.5 * parity / safe)


def mode_tables(points):
    indices = jnp.arange(points, dtype=jnp.int32)
    product = indices[:, None] * indices[None, :] % points
    angles = 2.0 * jnp.pi * product.astype(jnp.float32) / points
    return (jnp.cos(angles), jnp.sin(angles))


def cycle_response(points, cycle_index, near):
    indices = jnp.arange(points, dtype=jnp.int32)
    wave_number = jnp.minimum(indices, points - indices)
    cutoff = jnp.maximum(4, points * (cycle_index + 1) // (2 * near))
    return (wave_number[None, :] < cutoff[:, None]).astype(jnp.float32)


def smooth_cycles(pencil, first_cycle, near):
    points = pencil.shape[1]
    cycles = pencil.shape[2]
    cosines, sines_table = mode_tables(points)
    cycle_index = first_cycle + jnp.arange(cycles, dtype=jnp.int32)
    response = (cycle_response(points, cycle_index, near).T / points)[None, :, :, None]
    coef_cos = jnp.einsum("tk,ftrx->fkrx", cosines, pencil, precision=lax.Precision.HIGHEST)
    coef_sin = jnp.einsum("tk,ftrx->fkrx", sines_table, pencil, precision=lax.Precision.HIGHEST)
    smoothed = jnp.einsum(
        "tk,fkrx->ftrx", cosines, coef_cos * response, precision=lax.Precision.HIGHEST
    )
    smoothed = smoothed + jnp.einsum(
        "tk,fkrx->ftrx", sines_table, coef_sin * response, precision=lax.Precision.HIGHEST
    )
    weights = jnp.maximum(1.0 - cycle_index.astype(jnp.float32) / near, 0.0)[None, None, :, None]
    return pencil + weights * (smoothed - pencil)


def viscous(center, nbr_up, nbr_dn, visc, visc_up, visc_dn, kappa, flags):
    cycles = center.shape[2]
    cells_x = center.shape[3]
    cycle_weight = (1.0 / (jnp.arange(cycles, dtype=jnp.float32) + 1.0))[None, :, None]
    theta = cycle_weight * (
        0.5 * (visc + visc_up) * (center - nbr_up) + 0.5 * (visc + visc_dn) * (center - nbr_dn)
    )
    face_r = 0.5 * (visc[:, :-1, :] + visc[:, 1:, :])
    flux_r = face_r * (center[:, :, :-1, :] - center[:, :, 1:, :])
    radial = jnp.pad(flux_r, ((0, 0), (0, 0), (0, 1), (0, 0))) - jnp.pad(
        flux_r, ((0, 0), (0, 0), (1, 0), (0, 0))
    )
    face_x = 0.5 * (visc[:, :, :-1] + visc[:, :, 1:])
    flux_x = face_x * (center[:, :, :, :-1] - center[:, :, :, 1:])
    axial = jnp.pad(flux_x, ((0, 0), (0, 0), (0, 0), (0, 1))) - jnp.pad(
        flux_x, ((0, 0), (0, 0), (0, 0), (1, 0))
    )
    open_faces = (1 - flags).astype(jnp.float32)
    outer = open_faces[:, 2][:, None, None, None] * visc[None, :, -1:, :] * center[:, :, -1:, :]
    outer = jnp.pad(outer, ((0, 0), (0, 0), (cycles - 1, 0), (0, 0)))
    inflow = open_faces[:, 0][:, None, None, None] * visc[None, :, :, :1] * center[:, :, :, :1]
    inflow = jnp.pad(inflow, ((0, 0), (0, 0), (0, 0), (0, cells_x - 1)))
    outflow = open_faces[:, 1][:, None, None, None] * visc[None, :, :, -1:] * center[:, :, :, -1:]
    outflow = jnp.pad(outflow, ((0, 0), (0, 0), (0, 0), (cells_x - 1, 0)))
    return kappa[:, None, None, None] * (theta + radial + axial + outer + inflow + outflow)


def body(adjoint, source, viscosity, kappa, coupling, bc_flags, inst_map):
    slots = lax.axis_size("inst")
    own_slot = lax.axis_index("inst")
    matrix = spectral_matrix(inst_map, slots)
    center = adjoint[0]
    column = lax.dynamic_slice_in_dim(matrix, own_slot, 1, 1)[:, 0]
    spectral = jnp.tensordot(
        column,
        lax.all_gather(adjoint, "inst", axis=0, tiled=True),
        axes=1,
        precision=lax.Precision.HIGHEST,
    )
    stacked = jnp.concatenate([center, viscosity[None]], axis=0)
    padded = with_halo(stacked, (("space", 1),), 1)
    fields = center.shape[0]
    diffused = viscous(
        center,
        padded[:fields, 2:],
        padded[:fields, :-2],
        viscosity,
        padded[fields, 2:],
        padded[fields, :-2],
        kappa,
        bc_flags,
    )
    coupled = jnp.einsum("gf,gtrx->ftrx", coupling, center, precision=lax.Precision.HIGHEST)
    pre = source[0] + coupled + diffused + spectral
    total_cycles = pre.shape[2]
    near = total_cycles // 2
    pencil = lax.all_to_all(pre, "space", split_axis=2, concat_axis=1, tiled=True)
    first_cycle = lax.axis_index("space") * pencil.shape[2]
    result = smooth_cycles(pencil, first_cycle, near)
    residual = lax.all_to_all(result, "space", split_axis=1, concat_axis=2, tiled=True)
    return residual[None]


def solution(mesh):
    return jax.shard_map(
        body,
        mesh=mesh,
        in_specs=(
            P("inst", None, "space", None, None),
            P("inst", None, "space", None, None),
            P("space", None, None),
            P(),
            P(),
            P(),
            P(),
        ),
        out_specs=P("inst", None, "space", None, None),
        check_vma=False,
    )
```

profile of v0, /device:TPU:1, one launch (start us, length us, event | category | flops | bytes accessed | tf_op | source)
XLA Modules:
  0.0 362.0 jit_solution(16795134154637012902)
XLA Ops:
  6.5 0.7 all-gather.2.cloned.1.call-update
  7.3 0.6 copy-done.1
  7.9 1.6 fusion.36
  9.4 4.3 %collective-permute-start.1 = (f32[6,1,64,128]{3,2,1,0:T(8,128)}, f32[6,1,64,128]{3,2,1,0:T(8,128)}, u32[]{:S(2)}, u32[]{:S(2)}) collective-permute-start(f32[6,1,64,128]{3,2,1,0:T(8,128)} %get-tuple-element.8), channel_id=1, source_target_pairs={{0,1},{1,2},{2,3},{3,4},{4,5},{5,6},{6,7},{7,8},{8,9},{9,10},{10,1... | collective-permute-start | bytes 589832 | tf_op jit(solution)/shard_map/ppermute | solution.py:13
  13.7 0.8 copy.120
  14.5 0.8 slice.88
  15.3 1.9 fusion.78
  17.2 1.1 copy.102
  18.3 1.1 copy.103
  19.4 1.2 pad_maximum_fusion
  20.9 1.6 fusion.14
  22.5 2.0 fusion.2
  24.5 3.7 %slice_multiply_fusion.1 = (f32[5,8,64,1]{3,0,2,1:T(8,128)}, f32[5,8,64,1]{3,0,2,1:T(8,128)}) fusion(f32[5,8,64,128]{3,0,2,1:T(8,128)S(1)} %bitcast.91, f32[8,64]{1,0:T(8,128)S(1)} %bitcast.107, f32[5]{0:T(128)S(1)} %get-tuple-element.15, f32[8,64]{1,0:T(8,128)S(1)} %bitcast.108, f32[5]{0:T(128)S(1)} %get-tuple-element.14), kind=kLoop, calls=%fused_computation.6 | loop fusion | flops 10240 | bytes 45096 | tf_op jit(solution)/shard_map/mul | solution.py:81
  28.3 1.0 copy_dynamic-update-slice_fusion.1
  29.3 0.9 copy_dynamic-update-slice_fusion
  30.6 0.9 add_multiply_fusion.2
  31.7 1.1 fusion.22
  32.8 190.1 %all-gather.2.cloned.1.call-done = f32[8,5,8,64,128]{4,3,2,1,0:T(8,128)} async-done(((f32[1,5,8,64,128]{4,3,2,1,0:T(8,128)}), f32[8,5,8,64,128]{4,3,2,1,0:T(8,128)}) %all-gather.2.cloned.1.call-update) | async-done | bytes 10485776 | tf_op jit(solution)/shard_map/all_gather | solution.py:96
  223.0 19.2 %fusion = f32[1,5,8,64,128]{4,0,3,2,1:T(1,128)S(1)} fusion(f32[8,5,8,64,128]{4,3,2,1,0:T(8,128)} %all-gather.2.cloned.1.call-done, f32[8,8]{0,1:T(8,128)S(1)} %fusion.47, s32[]{:T(128)S(6)} %select_n.41), kind=kOutput, calls=%fused_computation | convolution fusion | flops 31457280 | bytes 11796996 | tf_op jit(solution)/shard_map/dot_general | solution.py:94
  242.3 8.9 %fusion.13 = f32[5,8,64,128]{3,0,2,1:T(8,128)S(1)} fusion(f32[6,9,64,128]{3,0,2,1:T(8,128)} %copy-done.9, f32[1,5,8,64,128]{4,0,3,2,1:T(1,128)S(1)} %fusion, f32[5,8,64,128]{3,2,1,0:T(8,128)S(1)} %fusion.22, f32[1,5,8,64,128]{4,3,2,1,0:T(8,128)S(1)} %copy-done.8, f32[5,8,64,1]{3,0,2,1:T(8,128)S(1)} %copy-done.5, f32[5,8,64,1]{3,0,2,1:T(8,128)S(1)} %copy-done.4, ...), kind=kOutput, calls=%fused_computation.20 | convolution fusion | flops 24576000 | bytes 17830912 | tf_op jit(solution)/shard_map/gf,gtrx->ftrx/dot_general | solution.py:113
  251.2 1.8 copy.79
  253.0 10.4 %all-to-all-start = ((f32[5,8,64,128]{3,1,0,2:T(8,128)}), f32[5,8,64,128]{3,1,0,2:T(8,128)S(1)}, u32[]{:S(2)}, u32[]{:S(2)}) async-start(f32[5,8,64,128]{3,1,0,2:T(8,128)} %copy.79), calls=%async_computation | async-start | bytes 2621440 | tf_op jit(solution)/shard_map/all_to_all | solution.py:117
  263.6 33.4 %all-to-all-done = f32[5,8,64,128]{3,1,0,2:T(8,128)S(1)} async-done(((f32[5,8,64,128]{3,1,0,2:T(8,128)}), f32[5,8,64,128]{3,1,0,2:T(8,128)S(1)}, u32[]{:S(2)}, u32[]{:S(2)}) %all-to-all-start) | async-done | bytes 1310752 | tf_op jit(solution)/shard_map/all_to_all | solution.py:117
  297.0 1.2 copy.121
  298.2 3.2 fusion.16
  301.4 4.2 %fusion.15 = f32[5,256,2,128]{1,3,2,0:T(8,128)} fusion(f32[256,2]{0,1:T(2,128)S(1)} %compare_select_fusion, f32[5,32,8,2,128]{4,2,0,3,1:T(8,128)S(1)} %bitcast.102), kind=kOutput, calls=%fused_computation.30 | convolution fusion | flops 1007878144 | bytes 2623488 | tf_op jit(solution)/shard_map/tk,ftrx->fkrx/dot_general | solution.py:50
  305.6 1.7 copy.85
  307.3 2.2 fusion.30
  309.5 2.3 fusion.20
  311.8 1.3 copy.86
  313.1 40.4 %all_to_all.33 = f32[5,256,2,128]{3,2,0,1:T(2,128)S(1)} all-to-all(f32[5,256,2,128]{3,2,0,1:T(2,128)S(1)} %copy.86), channel_id=1, replica_groups=mesh['inst'=8,'space'=32] {'space'}, dimensions={1} | all-to-all | bytes 2621440 | tf_op jit(solution)/shard_map/all_to_all | solution.py:120
  353.7 1.3 copy.89
  (43 shorter events, 1.3 us)
Async XLA Ops:
  6.5 235.7 %copy-start = (f32[5,5]{1,0:T(8,128)S(1)}, f32[5,5]{1,0:T(8,128)}, u32[]{:S(2)}) copy-start(f32[5,5]{1,0:T(8,128)} %param.11) | copy-start | bytes 304
  6.5 1.3 copy-start.1
  6.5 216.4 %all-gather.2.cloned.1.call-start = ((), (), s32[]{:S(2)}) async-start(), calls=%async_computation.2 | async-start | bytes 11796480 | tf_op jit(solution)/shard_map/all_gather | solution.py:96
  9.4 18.8 %collective-permute-start.1 = (f32[6,1,64,128]{3,2,1,0:T(8,128)}, f32[6,1,64,128]{3,2,1,0:T(8,128)}, u32[]{:S(2)}, u32[]{:S(2)}) collective-permute-start(f32[6,1,64,128]{3,2,1,0:T(8,128)} %get-tuple-element.8), channel_id=1, source_target_pairs={{0,1},{1,2},{2,3},{3,4},{4,5},{5,6},{6,7},{7,8},{8,9},{9,10},{10,1... | collective-permute-start | bytes 589832 | tf_op jit(solution)/shard_map/ppermute | solution.py:13
  13.7 16.8 %collective-permute-start = (f32[6,1,64,128]{3,2,1,0:T(8,128)}, f32[6,1,64,128]{3,2,1,0:T(8,128)}, u32[]{:S(2)}, u32[]{:S(2)}) collective-permute-start(f32[6,1,64,128]{3,2,1,0:T(8,128)} %get-tuple-element.7), channel_id=1, source_target_pairs={{1,0},{2,1},{3,2},{4,3},{5,4},{6,5},{7,6},{8,7},{9,8},{10,9},{11,1... | collective-permute-start | bytes 589832 | tf_op jit(solution)/shard_map/ppermute | solution.py:16
  17.2 3.4 copy-start.11
  19.3 1.4 copy-start.2
  24.5 3.7 %copy-start.10 = (s32[8]{0:T(128)S(1)}, s32[8]{0:T(128)}, u32[]{:S(2)}) copy-start(s32[8]{0:T(128)} %param.13) | copy-start | bytes 100
  30.3 1.5 copy-start.9
  32.8 209.4 %copy-start.12 = (f32[5]{0:T(128)S(1)}, f32[5]{0:T(128)}, u32[]{:S(2)}) copy-start(f32[5]{0:T(128)} %param.10) | copy-start | bytes 64
  223.0 19.3 %copy-start.3 = (f32[5,8,64,127]{3,0,2,1:T(8,128)S(1)}, f32[5,8,64,127]{3,0,2,1:T(8,128)}, u32[]{:S(2)}) copy-start(f32[5,8,64,127]{3,0,2,1:T(8,128)} %fusion.2) | copy-start | bytes 3901444
  223.0 19.3 %copy-start.4 = (f32[5,8,64,1]{3,0,2,1:T(8,128)S(1)}, f32[5,8,64,1]{3,0,2,1:T(8,128)}, u32[]{:S(2)}) copy-start(f32[5,8,64,1]{3,0,2,1:T(8,128)} %get-tuple-element.5) | copy-start | bytes 30724
  223.0 19.3 %copy-start.5 = (f32[5,8,64,1]{3,0,2,1:T(8,128)S(1)}, f32[5,8,64,1]{3,0,2,1:T(8,128)}, u32[]{:S(2)}) copy-start(f32[5,8,64,1]{3,0,2,1:T(8,128)} %get-tuple-element.6) | copy-start | bytes 30724
  223.0 19.3 %copy-start.6 = (f32[5,8,63,128]{3,0,2,1:T(8,128)S(1)}, f32[5,8,63,128]{3,0,2,1:T(8,128)}, u32[]{:S(2)}) copy-start(f32[5,8,63,128]{3,0,2,1:T(8,128)} %fusion.14) | copy-start | bytes 3870724
  223.0 19.3 %copy-start.8 = (f32[1,5,8,64,128]{4,3,2,1,0:T(8,128)S(1)}, f32[1,5,8,64,128]{4,3,2,1,0:T(8,128)}, u32[]{:S(2)}) copy-start(f32[1,5,8,64,128]{4,3,2,1,0:T(8,128)} %param.8) | copy-start | bytes 3932164
  253.0 44.0 %all-to-all-start = ((f32[5,8,64,128]{3,1,0,2:T(8,128)}), f32[5,8,64,128]{3,1,0,2:T(8,128)S(1)}, u32[]{:S(2)}, u32[]{:S(2)}) async-start(f32[5,8,64,128]{3,1,0,2:T(8,128)} %copy.79), calls=%async_computation | async-start | bytes 2621440 | tf_op jit(solution)/shard_map/all_to_all | solution.py:117
  307.3 2.2 copy-start.7
Sparse Core Ops, SparseCore 0:
  9.1 213.7 all-gather.1
where the time goes:
time: 368 us; the launch traced here: 362 us
  waiting for transfers between devices  224 us (61%)
  blocking collectives  40.4 us (11%)
  matrix products  40 us (11%)
  local copies, waits for them, and re-layouts  16.2 us (4%)
  starting transfers between devices  14.7 us (4%)
  between operations  13.9 us (4%)
  other arithmetic  12.5 us (3%)
    all_gather x1, waiting for transfers between devices, body(): lax.all_gather(adjoint, 'inst', axis=0, tiled=True)  190 us
    all_to_all x1, blocking collectives, body(): lax.all_to_all(result, 'space', split_axis=1, concat_axis=2, tiled=True)  40.4 us
    all_to_all x1, waiting for transfers between devices, body(): lax.all_to_all(pre, 'space', split_axis=2, concat_axis=1, tiled=True)  33.4 us
    dot_general x1, matrix products, body(): jnp.tensordot(column, lax.all_gather(adjoint, 'inst', axis=0, tiled=True)...  19.2 us
    all_to_all x1, starting transfers between devices, body(): lax.all_to_all(pre, 'space', split_axis=2, concat_axis=1, tiled=True)  10.4 us
    dot_general x1, matrix products, body(): jnp.einsum('gf,gtrx->ftrx', coupling, center, precision=lax.Precision.HIG...  8.9 us
  transfers between devices with their start and end apart: 4, of which 2 were waited for; matrix products, arithmetic and copies ran while one was open for 6% of the time, Pallas kernels for 0%

commit v1 on v0

v1 whole, which is shorter than its diff:
```python
import functools

import jax
import jax.numpy as jnp
import numpy as np
from jax import lax
from jax.experimental import pallas as pl
from jax.experimental.pallas import tpu as pltpu
from jax.sharding import PartitionSpec as P

FIELDS, SECTOR, CYCLES, CELLS_X = 5, 8, 64, 128
POINTS, NEAR, SLOTS, SECTORS = 256, 32, 8, 32
GROUPS = ((0, 2), (2, 5))
MESH = pl.DeviceIdType.MESH


def slot_table():
    offset = np.arange(-(SLOTS - 1), SLOTS + 1)
    parity = 1.0 - 2.0 * (np.abs(offset) % 2)
    sines = np.sin(np.pi * offset / SLOTS)
    inner = (offset != 0) & (np.abs(offset) < SLOTS)
    table = np.where(inner, 0.5 * parity / np.where(inner, sines, 1.0), 0.0)
    return jnp.asarray(table.astype(np.float32))


def kernel(adj, src, visc, kap, cpl, bcf, imap, tab, out, *scratch):
    count = len(GROUPS)
    names = iter(scratch)
    take = lambda n: [next(names) for _ in range(n)]
    adjx, mux, local, outv, mtab = take(5)
    recv_a = take(count + 1)
    mixed = take(count + 1)
    spec = take(count + 1)
    stage_e, recv_e, stage_g, recv_g = take(count), take(count), take(count), take(count)
    load_sem, halo_send, halo_recv, own_sem, out_sem = take(5)
    a_send, a_recv, c_send, c_recv = take(4)
    e_send, e_recv, g_send, g_recv = take(4)

    me, sp = lax.axis_index("inst"), lax.axis_index("space")
    ix, iy = lax.div(me, 2), lax.rem(me, 2)
    sz, sy, sc = lax.div(sp, 4), lax.rem(lax.div(sp, 2), 2), lax.rem(sp, 2)

    def inst_at(k, sign):
        kx, ky = k // 2, k % 2
        return lax.rem(ix + sign * kx + 4, 4) * 2 + lax.rem(iy + ky, 2)

    def space_at(i, sign):
        step = lax.div(i, 4)
        kz = lax.div(step + 1, 2) * (1 - 2 * lax.rem(step, 2))
        return (
            lax.rem(sz + sign * kz + 8, 8) * 4
            + lax.rem(sy + lax.rem(lax.div(i, 2), 2), 2) * 2
            + lax.rem(sc + lax.rem(i, 2), 2)
        )

    loads = [
        pltpu.make_async_copy(visc, mux.at[pl.ds(1, SECTOR)], load_sem.at[0]),
        pltpu.make_async_copy(adj.at[0], adjx.at[:, pl.ds(1, SECTOR)], load_sem.at[1]),
        pltpu.make_async_copy(src.at[0], local, load_sem.at[2]),
    ]
    bounds = [(lo, hi, 0) for lo, hi in GROUPS] + [(0, FIELDS, NEAR)]

    def chunk(g, slot):
        lo, hi, first = bounds[g]
        return adj.at[0, pl.ds(lo, hi - lo), slot, pl.ds(first, NEAR), :]

    own_a = [
        pltpu.make_async_copy(chunk(g, me), recv_a[g].at[me], own_sem.at[0, g])
        for g in range(count + 1)
    ]
    own_c = [
        pltpu.make_async_copy(mixed[g].at[me], spec[g].at[:, me], own_sem.at[1, g])
        for g in range(count + 1)
    ]

    def rows(g, index):
        depth = (bounds[g][1] - bounds[g][0]) * SECTOR
        return pl.ds(pl.multiple_of(index * depth, 8), depth)

    own_e = [
        pltpu.make_async_copy(
            stage_e[g].at[rows(g, sp)], recv_e[g].at[rows(g, sp)], own_sem.at[2, g]
        )
        for g in range(count)
    ]
    own_g = [
        pltpu.make_async_copy(
            stage_g[g].at[rows(g, sp)], recv_g[g].at[rows(g, sp)], own_sem.at[3, g]
        )
        for g in range(count)
    ]

    def send_a(g, k):
        return pltpu.make_async_remote_copy(
            src_ref=chunk(g, inst_at(k, 1)),
            dst_ref=recv_a[g].at[me],
            send_sem=a_send.at[g, k],
            recv_sem=a_recv.at[g, k],
            device_id={"inst": inst_at(k, 1)},
            device_id_type=MESH,
        )

    def arrive_a(g, k):
        return pltpu.make_async_remote_copy(
            src_ref=chunk(g, me),
            dst_ref=recv_a[g].at[inst_at(k, -1)],
            send_sem=a_send.at[g, k],
            recv_sem=a_recv.at[g, k],
            device_id={"inst": inst_at(k, 1)},
            device_id_type=MESH,
        )

    def send_c(g, k):
        return pltpu.make_async_remote_copy(
            src_ref=mixed[g].at[inst_at(k, 1)],
            dst_ref=spec[g].at[:, me],
            send_sem=c_send.at[g, k],
            recv_sem=c_recv.at[g, k],
            device_id={"inst": inst_at(k, 1)},
            device_id_type=MESH,
        )

    def arrive_c(g, k):
        return pltpu.make_async_remote_copy(
            src_ref=mixed[g].at[me],
            dst_ref=spec[g].at[:, inst_at(k, -1)],
            send_sem=c_send.at[g, k],
            recv_sem=c_recv.at[g, k],
            device_id={"inst": inst_at(k, 1)},
            device_id_type=MESH,
        )

    def send_s(stage, recv, send_sem, recv_sem, g, i, slot):
        return pltpu.make_async_remote_copy(
            src_ref=stage[g].at[rows(g, space_at(i, 1))],
            dst_ref=recv[g].at[rows(g, slot)],
            send_sem=send_sem.at[g, i],
            recv_sem=recv_sem.at[g, i],
            device_id={"space": space_at(i, 1)},
            device_id_type=MESH,
        )

    after, before = lax.rem(sp + 1, SECTORS), lax.rem(sp + SECTORS - 1, SECTORS)

    def halo(index, source, target, peer):
        return pltpu.make_async_remote_copy(
            src_ref=source,
            dst_ref=target,
            send_sem=halo_send.at[index],
            recv_sem=halo_recv.at[index],
            device_id={"space": peer},
            device_id_type=MESH,
        )

    halos = [
        halo(0, adj.at[0, :, SECTOR - 1], adjx.at[:, 0], after),
        halo(1, adj.at[0, :, 0], adjx.at[:, SECTOR + 1], before),
        halo(2, visc.at[SECTOR - 1], mux.at[0], after),
        halo(3, visc.at[0], mux.at[SECTOR + 1], before),
    ]

    barrier = pltpu.get_barrier_semaphore()
    for k in range(1, SLOTS):
        pl.semaphore_signal(
            barrier, inc=1, device_id={"inst": inst_at(k, 1)}, device_id_type=MESH
        )

    @pl.loop(1, SECTORS)
    def _(i):
        pl.semaphore_signal(
            barrier, inc=1, device_id={"space": space_at(i, 1)}, device_id_type=MESH
        )

    for copy in loads:
        copy.start()
    for copy in own_a:
        copy.start()
    pl.semaphore_wait(barrier, SLOTS - 1 + SECTORS - 1)

    for g in range(count):
        for k in range(1, SLOTS):
            send_a(g, k).start()
        if g == 0:
            for copy in halos:
                copy.start()

    cutoff = jnp.maximum(4, lax.div(POINTS * (sp + 1), 2 * NEAR))
    width = 2 * cutoff - 1
    weight = 1.0 - sp.astype(jnp.float32) / NEAR

    @pl.loop(0, POINTS // 32)
    def _(b):
        row = lax.broadcasted_iota(jnp.int32, (32, POINTS), 0) + b * 32
        col = lax.broadcasted_iota(jnp.int32, (32, POINTS), 1)
        gap = (row - col + POINTS) & (POINTS - 1)
        top = jnp.sin(((gap * width) & (2 * POINTS - 1)).astype(jnp.float32) * (np.pi / POINTS))
        low = jnp.sin(gap.astype(jnp.float32) * (np.pi / POINTS))
        same = gap == 0
        ratio = top / jnp.where(same, 1.0, low)
        table = jnp.where(same, width.astype(jnp.float32), ratio) * (1.0 / POINTS)
        mtab[pl.ds(pl.multiple_of(b * 32, 32), 32), :] = weight * table + jnp.where(
            same, 1.0 - weight, 0.0
        )

    def mix(g):
        own_a[g].wait()
        for k in range(1, SLOTS):
            arrive_a(g, k).wait_recv()
        fields = bounds[g][1] - bounds[g][0]
        coef = {
            (j, n): tab[imap[j] - imap[n] + SLOTS - 1]
            for n in range(SLOTS)
            for j in range(n + 1, SLOTS)
        }

        @pl.loop(0, fields * NEAR // 8)
        def _(b):
            fi, r0 = lax.div(b, NEAR // 8), lax.rem(b, NEAR // 8) * 8
            block = pl.ds(pl.multiple_of(r0, 8), 8)
            values = [recv_a[g][j, fi, block, :] for j in range(SLOTS)]
            for n in range(SLOTS):
                total = None
                for j in range(SLOTS):
                    if j == n:
                        continue
                    term = coef[max(j, n), min(j, n)] * values[j]
                    if total is None:
                        total = term if j > n else -term
                    else:
                        total = total + term if j > n else total - term
                mixed[g][n, fi, block, :] = total

        for k in range(1, SLOTS):
            send_c(g, k).start()
        own_c[g].start()

    for g in range(count):
        mix(g)
    for k in range(1, SLOTS):
        send_a(count, k).start()

    for copy in loads:
        copy.wait()
    for copy in halos:
        copy.wait_recv()

    row = lax.broadcasted_iota(jnp.int32, (CYCLES, CELLS_X), 0)
    col = lax.broadcasted_iota(jnp.int32, (CYCLES, CELLS_X), 1)

    @pl.loop(0, SECTOR)
    def _(t):
        mu = mux[t + 1]
        half_cycle = 0.5 / (row.astype(jnp.float32) + 1.0)
        up = half_cycle * (mu + mux[t + 2])
        down = half_cycle * (mu + mux[t])
        out_r = jnp.where(
            row < CYCLES - 1, 0.5 * (mu + pltpu.roll(mu, CYCLES - 1, 0)), 0.0
        )
        in_r = pltpu.roll(out_r, 1, 0)
        out_x = jnp.where(
            col < CELLS_X - 1, 0.5 * (mu + pltpu.roll(mu, CELLS_X - 1, 1)), 0.0
        )
        in_x = pltpu.roll(out_x, 1, 1)
        own = up + down + out_r + in_r + out_x + in_x
        for f in range(FIELDS):
            p = adjx[f, t + 1]
            face = [1.0 - bcf[f, i].astype(jnp.float32) for i in range(3)]
            edge = (
                jnp.where(row == CYCLES - 1, face[2], 0.0)
                + jnp.where(col == 0, face[0], 0.0)
                + jnp.where(col == CELLS_X - 1, face[1], 0.0)
            )
            diffused = (own + edge * mu) * p
            diffused = diffused - up * adjx[f, t + 2] - down * adjx[f, t]
            diffused = diffused - out_r * pltpu.roll(p, CYCLES - 1, 0)
            diffused = diffused - in_r * pltpu.roll(p, 1, 0)
            diffused = diffused - out_x * pltpu.roll(p, CELLS_X - 1, 1)
            diffused = diffused - in_x * pltpu.roll(p, 1, 1)
            total = local[f, t] + kap[f] * diffused
            for g in range(FIELDS):
                total = total + cpl[g, f] * adjx[g, t + 1]
            local[f, t] = total

    for g in range(count):
        lo, hi, _ = bounds[g]
        own_c[g].wait()
        for k in range(1, SLOTS):
            arrive_c(g, k).wait_recv()
        stride = (hi - lo) * SECTOR

        @pl.loop(0, SECTOR)
        def _(t):
            for f in range(lo, hi):
                for b in range(NEAR // 8):
                    block = pl.ds(b * 8, 8)
                    value = local[f, t, block, :] + spec[g][f - lo, t, block, :]
                    start = b * 8 * stride + (f - lo) * SECTOR + t
                    stage_e[g][pl.ds(start, 8, stride=stride), :] = value

        own_e[g].start()

        @pl.loop(1, SECTORS)
        def _(i):
            send_s(stage_e, recv_e, e_send, e_recv, g, SECTORS - i, sp).start()

    mix(count)

    for g in range(count):
        lo, hi, _ = bounds[g]
        own_e[g].wait()

        @pl.loop(1, SECTORS)
        def _(i):
            send_s(
                stage_e, recv_e, e_send, e_recv, g, SECTORS - i, space_at(SECTORS - i, -1)
            ).wait_recv()

        pencils = recv_e[g][...].reshape(SECTORS, (hi - lo) * SECTOR, CELLS_X)
        parts = []
        for f in range(hi - lo):
            pencil = pencils[:, f * SECTOR : (f + 1) * SECTOR, :].reshape(POINTS, CELLS_X)
            smooth = jnp.dot(
                mtab[...],
                pencil,
                precision=lax.Precision.HIGHEST,
                preferred_element_type=jnp.float32,
            )
            parts.append(smooth.reshape(SECTORS, SECTOR, CELLS_X))
        stage_g[g][...] = jnp.concatenate(parts, axis=1).reshape(
            SECTORS * (hi - lo) * SECTOR, CELLS_X
        )
        own_g[g].start()

        @pl.loop(1, SECTORS)
        def _(i):
            send_s(stage_g, recv_g, g_send, g_recv, g, SECTORS - i, sp).start()

    own_c[count].wait()
    for k in range(1, SLOTS):
        arrive_c(count, k).wait_recv()

    @pl.loop(0, SECTOR)
    def _(t):
        for f in range(FIELDS):
            outv[f, t, pl.ds(NEAR, NEAR), :] = (
                local[f, t, pl.ds(NEAR, NEAR), :] + spec[count][f, t]
            )

    far = pltpu.make_async_copy(
        outv.at[:, :, pl.ds(NEAR, NEAR), :],
        out.at[0, :, :, pl.ds(NEAR, NEAR), :],
        out_sem.at[count],
    )
    far.start()
    writes = [far]

    for g in range(count):
        lo, hi, _ = bounds[g]
        own_g[g].wait()

        @pl.loop(1, SECTORS)
        def _(i):
            send_s(
                stage_g, recv_g, g_send, g_recv, g, SECTORS - i, space_at(SECTORS - i, -1)
            ).wait_recv()

        stride = (hi - lo) * SECTOR

        @pl.loop(0, SECTOR)
        def _(t):
            for f in range(lo, hi):
                for b in range(NEAR // 8):
                    start = b * 8 * stride + (f - lo) * SECTOR + t
                    outv[f, t, pl.ds(b * 8, 8), :] = recv_g[g][
                        pl.ds(start, 8, stride=stride), :
                    ]

        write = pltpu.make_async_copy(
            outv.at[pl.ds(lo, hi - lo), :, pl.ds(0, NEAR), :],
            out.at[0, pl.ds(lo, hi - lo), :, pl.ds(0, NEAR), :],
            out_sem.at[g],
        )
        write.start()
        writes.append(write)

    for copy in halos:
        copy.wait_send()
    for g in range(count + 1):
        for k in range(1, SLOTS):
            send_a(g, k).wait_send()
            send_c(g, k).wait_send()
    for g in range(count):

        @pl.loop(1, SECTORS)
        def _(i):
            send_s(stage_e, recv_e, e_send, e_recv, g, SECTORS - i, sp).wait_send()
            send_s(stage_g, recv_g, g_send, g_recv, g, SECTORS - i, sp).wait_send()

    for copy in writes:
        copy.wait()


def body(adjoint, source, viscosity, kappa, coupling, bc_flags, inst_map):
    count = len(GROUPS)
    sizes = [hi - lo for lo, hi in GROUPS]
    f32 = jnp.float32
    vmem, dma = pltpu.VMEM, pltpu.SemaphoreType.DMA
    slabs = [vmem((SLOTS, n, NEAR, CELLS_X), f32) for n in sizes + [FIELDS]]
    sectors = [vmem((n, SECTOR, NEAR, CELLS_X), f32) for n in sizes + [FIELDS]]
    pencils = [vmem((SECTORS * n * SECTOR, CELLS_X), f32) for n in sizes]
    scratch = [
        vmem((FIELDS, SECTOR + 2, CYCLES, CELLS_X), f32),
        vmem((SECTOR + 2, CYCLES, CELLS_X), f32),
        vmem((FIELDS, SECTOR, CYCLES, CELLS_X), f32),
        vmem((FIELDS, SECTOR, CYCLES, CELLS_X), f32),
        vmem((POINTS, POINTS), f32),
        *slabs,
        *slabs,
        *sectors,
        *(pencils * 4),
        dma((3,)),
        dma((4,)),
        dma((4,)),
        dma((4, count + 1)),
        dma((count + 1,)),
        *[dma((count + 1, SLOTS))] * 4,
        *[dma((count, SECTORS))] * 4,
    ]
    hbm, smem = pl.BlockSpec(memory_space=pl.ANY), pl.BlockSpec(memory_space=pltpu.SMEM)
    return pl.pallas_call(
        kernel,
        out_shape=jax.ShapeDtypeStruct(adjoint.shape, f32),
        in_specs=[hbm] * 3 + [smem] * 5,
        out_specs=hbm,
        scratch_shapes=scratch,
        compiler_params=pltpu.CompilerParams(
            collective_id=0, has_side_effects=True, vmem_limit_bytes=48 * 1024 * 1024
        ),
        name="residual",
    )(adjoint, source, viscosity, kappa, coupling, bc_flags, inst_map, slot_table())


def solution(mesh):
    return jax.shard_map(
        body,
        mesh=mesh,
        in_specs=(
            P("inst", None, "space", None, None),
            P("inst", None, "space", None, None),
            P("space", None, None),
            P(),
            P(),
            P(),
            P(),
        ),
        out_specs=P("inst", None, "space", None, None),
        check_vma=False,
    )
```

time: 368 us -> 87.6 us (0.24); the launches traced: 362 us -> 86.2 us
  waiting for transfers between devices: 224 us -> 0 us
  Pallas kernels: 0 us -> 78.2 us
  blocking collectives: 40.4 us -> 0 us
  matrix products: 40 us -> 0 us
  starting transfers between devices: 14.7 us -> 0 us
  between operations: 13.9 us -> 0.02 us
  other arithmetic: 12.5 us -> 0 us
  local copies, waits for them, and re-layouts: 16.2 us -> 8.06 us
    all_gather x1 -> x0, waiting for transfers between devices: 190 us -> none  [body(): lax.all_gather(adjoint, 'inst', axis=0, tiled=True)]
    pallas_call x0 -> x1, Pallas kernels: none -> 78.2 us  [body(): pl.pallas_call(kernel, out_shape=jax.ShapeDtypeStruct(adjoint.shape, f32)...]
    all_to_all x1 -> x0, blocking collectives: 40.4 us -> none  [body(): lax.all_to_all(result, 'space', split_axis=1, concat_axis=2, tiled=True)]
    dot_general x6 -> x0, matrix products: 40 us -> none  [the longest x1 19.2 us: body(): jnp.tensordot(column, lax.all_gather(adjoint, 'inst', axis=0, tiled=True)...]
    all_to_all x1 -> x0, waiting for transfers between devices: 33.4 us -> none  [body(): lax.all_to_all(pre, 'space', split_axis=2, concat_axis=1, tiled=True)]
    all_to_all x1 -> x0, starting transfers between devices: 10.4 us -> none  [body(): lax.all_to_all(pre, 'space', split_axis=2, concat_axis=1, tiled=True)]
    mul x8 -> x0, other arithmetic: 9.46 us -> none  [the longest x1 3.68 us: viscous(): open_faces[:, 0][:, None, None, None] * visc[None, :, :, :1]]
    ppermute x2 -> x0, starting transfers between devices: 4.3 us -> none  [the longest x1 4.29 us: with_halo(): lax.ppermute(lax.slice_in_dim(block, block.shape[dim] - width, None, axis...]
  transfers between devices with their start and end apart: 4 -> 0, of which waited for: 2 -> 0; matrix products, arithmetic and copies ran while one was open for 6% -> 0% of each run, Pallas kernels for 0% -> 0%
where the time goes in v1:
time: 87.6 us; the launch traced here: 86.2 us
  Pallas kernels  78.2 us (89%)
  local copies, waits for them, and re-layouts  8.06 us (9%)
    pallas_call x1, Pallas kernels, body(): pl.pallas_call(kernel, out_shape=jax.ShapeDtypeStruct(adjoint.shape, f32)...  78.2 us
    unnamed x16, local copies, waits for them, and re-layouts  8.06 us

profile of v1, /device:TPU:1, one launch (start us, length us, event | category | flops | bytes accessed | tf_op | source)
XLA Modules:
  0.0 86.2 jit_solution(7058960675754588723)
XLA Ops:
  0.0 0.8 copy.9.bcf
  0.8 0.0 copy-start
  0.8 1.3 %copy-done = f32[1,5,8,64,128]{4,3,2,1,0:T(8,128)S(1)} copy-done((f32[1,5,8,64,128]{4,3,2,1,0:T(8,128)S(1)}, f32[1,5,8,64,128]{4,3,2,1,0:T(8,128)}, u32[]{:S(2)}) %copy-start) | copy-done | bytes 1310744
  2.1 0.0 copy-start.1
  2.1 1.3 %copy-done.1 = f32[1,5,8,64,128]{4,3,2,1,0:T(8,128)S(1)} copy-done((f32[1,5,8,64,128]{4,3,2,1,0:T(8,128)S(1)}, f32[1,5,8,64,128]{4,3,2,1,0:T(8,128)}, u32[]{:S(2)}) %copy-start.1) | copy-done | bytes 1310744
  3.4 0.0 copy-start.2
  3.4 0.9 %copy-done.2 = f32[8,64,128]{2,1,0:T(8,128)S(1)} copy-done((f32[8,64,128]{2,1,0:T(8,128)S(1)}, f32[8,64,128]{2,1,0:T(8,128)}, u32[]{:S(2)}) %copy-start.2) | copy-done | bytes 262168
  4.4 0.0 copy-start.3
  4.4 0.7 copy-done.3
  5.0 0.0 copy-start.4
  5.0 0.7 copy-done.4
  5.7 0.0 copy-start.5
  5.7 0.7 copy-done.5
  6.4 0.0 copy-start.6
  6.4 0.7 copy-done.6
  7.0 78.2 %residual.1 = f32[1,5,8,64,128]{4,3,2,1,0:T(8,128)S(1)} custom-call(f32[1,5,8,64,128]{4,3,2,1,0:T(8,128)S(1)} %copy-done, f32[1,5,8,64,128]{4,3,2,1,0:T(8,128)S(1)} %copy-done.1, f32[8,64,128]{2,1,0:T(8,128)S(1)} %copy-done.2, f32[5]{0:T(128)S(1)} %copy-done.4, f32[5,5]{1,0:T(8,128)S(1)} %copy-done.3, s32[5,3]{1,0:T(8,128)S(1)} %copy.9.bcf, s32[8]{0:T(128)S(1)} %copy-done.5, ...), custom_call_target="tpu_custom_call" | custom-call | tf_op jit(solution)/shard_map/residual/pallas_call | solution.py:430
  85.2 1.1 %copy.11 = f32[1,5,8,64,128]{4,3,2,1,0:T(8,128)} copy(f32[1,5,8,64,128]{4,3,2,1,0:T(8,128)S(1)} %residual.1) | data formatting | bytes 2621440
Async XLA Ops:
  0.8 1.3 %copy-start = (f32[1,5,8,64,128]{4,3,2,1,0:T(8,128)S(1)}, f32[1,5,8,64,128]{4,3,2,1,0:T(8,128)}, u32[]{:S(2)}) copy-start(f32[1,5,8,64,128]{4,3,2,1,0:T(8,128)} %adj.1) | copy-start | bytes 3932164
  2.1 1.3 %copy-start.1 = (f32[1,5,8,64,128]{4,3,2,1,0:T(8,128)S(1)}, f32[1,5,8,64,128]{4,3,2,1,0:T(8,128)}, u32[]{:S(2)}) copy-start(f32[1,5,8,64,128]{4,3,2,1,0:T(8,128)} %src.1) | copy-start | bytes 3932164
  3.4 0.9 %copy-start.2 = (f32[8,64,128]{2,1,0:T(8,128)S(1)}, f32[8,64,128]{2,1,0:T(8,128)}, u32[]{:S(2)}) copy-start(f32[8,64,128]{2,1,0:T(8,128)} %visc.1) | copy-start | bytes 786436
  4.4 0.7 copy-start.3
  5.0 0.7 copy-start.4
  5.7 0.7 copy-start.5
  6.4 0.7 copy-start.6

commit v2 on v1

--- a/solution.py
+++ b/solution.py
@@ -23,16 +23,19 @@
     return jnp.asarray(table.astype(np.float32))
 
 
-def kernel(adj, src, visc, kap, cpl, bcf, imap, tab, out, *scratch):
+def kernel(adj, src, visc, *refs):
+    smalls, out, scratch = refs[:5], refs[5], refs[6:]
     count = len(GROUPS)
     names = iter(scratch)
     take = lambda n: [next(names) for _ in range(n)]
-    adjx, mux, local, outv, mtab = take(5)
+    adjx, mux, local, mtab = take(4)
     recv_a = take(count + 1)
     mixed = take(count + 1)
     spec = take(count + 1)
     stage_e, recv_e, stage_g, recv_g = take(count), take(count), take(count), take(count)
-    load_sem, halo_send, halo_recv, own_sem, out_sem = take(5)
+    load_sem, halo_send, halo_recv, own_sem = take(4)
+    held = take(5)
+    kap, cpl, bcf, imap, tab = held
     a_send, a_recv, c_send, c_recv = take(4)
     e_send, e_recv, g_send, g_recv = take(4)
 
@@ -40,23 +43,28 @@
     ix, iy = lax.div(me, 2), lax.rem(me, 2)
     sz, sy, sc = lax.div(sp, 4), lax.rem(lax.div(sp, 2), 2), lax.rem(sp, 2)
 
+    flip_y = [iy, lax.rem(iy + 1, 2)]
+    turn_x = [lax.rem(ix + k, 4) * 2 for k in range(4)]
+    turn_z = [lax.rem(sz + k, 8) * 4 for k in range(8)]
+    flip_s = [sy * 2, lax.rem(sy + 1, 2) * 2]
+    flip_c = [sc, lax.rem(sc + 1, 2)]
+
     def inst_at(k, sign):
-        kx, ky = k // 2, k % 2
-        return lax.rem(ix + sign * kx + 4, 4) * 2 + lax.rem(iy + ky, 2)
+        return turn_x[(sign * (k // 2)) % 4] + flip_y[k % 2]
 
     def space_at(i, sign):
-        step = lax.div(i, 4)
-        kz = lax.div(step + 1, 2) * (1 - 2 * lax.rem(step, 2))
-        return (
-            lax.rem(sz + sign * kz + 8, 8) * 4
-            + lax.rem(sy + lax.rem(lax.div(i, 2), 2), 2) * 2
-            + lax.rem(sc + lax.rem(i, 2), 2)
-        )
+        step = i // 4
+        kz = (step + 1) // 2 * (1 - 2 * (step % 2))
+        return turn_z[(sign * kz) % 8] + flip_s[i // 2 % 2] + flip_c[i % 2]
 
     loads = [
         pltpu.make_async_copy(visc, mux.at[pl.ds(1, SECTOR)], load_sem.at[0]),
         pltpu.make_async_copy(adj.at[0], adjx.at[:, pl.ds(1, SECTOR)], load_sem.at[1]),
         pltpu.make_async_copy(src.at[0], local, load_sem.at[2]),
+    ]
+    consts = [
+        pltpu.make_async_copy(small, ref, load_sem.at[3 + i])
+        for i, (small, ref) in enumerate(zip(smalls, held))
     ]
     bounds = [(lo, hi, 0) for lo, hi in GROUPS] + [(0, FIELDS, NEAR)]
 
@@ -152,12 +160,17 @@
             device_id_type=MESH,
         )
 
-    halos = [
-        halo(0, adj.at[0, :, SECTOR - 1], adjx.at[:, 0], after),
-        halo(1, adj.at[0, :, 0], adjx.at[:, SECTOR + 1], before),
-        halo(2, visc.at[SECTOR - 1], mux.at[0], after),
-        halo(3, visc.at[0], mux.at[SECTOR + 1], before),
-    ]
+    def halos_of(part):
+        span = pl.ds(part * NEAR, NEAR)
+        first, last = SECTOR - 1, SECTOR + 1
+        return [
+            halo(4 * part, adj.at[0, :, first, span], adjx.at[:, 0, span], after),
+            halo(4 * part + 1, adj.at[0, :, 0, span], adjx.at[:, last, span], before),
+            halo(4 * part + 2, visc.at[first, span], mux.at[0, span], after),
+            halo(4 * part + 3, visc.at[0, span], mux.at[last, span], before),
+        ]
+
+    halos = [halos_of(0), halos_of(1)]
 
     barrier = pltpu.get_barrier_semaphore()
     for k in range(1, SLOTS):
@@ -165,13 +178,12 @@
             barrier, inc=1, device_id={"inst": inst_at(k, 1)}, device_id_type=MESH
         )
 
-    @pl.loop(1, SECTORS)
-    def _(i):
+    for i in range(SECTORS - 1, 0, -1):
         pl.semaphore_signal(
             barrier, inc=1, device_id={"space": space_at(i, 1)}, device_id_type=MESH
         )
 
-    for copy in loads:
+    for copy in consts + loads:
         copy.start()
     for copy in own_a:
         copy.start()
@@ -180,9 +192,8 @@
     for g in range(count):
         for k in range(1, SLOTS):
             send_a(g, k).start()
-        if g == 0:
-            for copy in halos:
-                copy.start()
+    for copy in halos[0]:
+        copy.start()
 
     cutoff = jnp.maximum(4, lax.div(POINTS * (sp + 1), 2 * NEAR))
     width = 2 * cutoff - 1
@@ -234,52 +245,63 @@
             send_c(g, k).start()
         own_c[g].start()
 
+    for copy in consts:
+        copy.wait()
     for g in range(count):
         mix(g)
-    for k in range(1, SLOTS):
-        send_a(count, k).start()
 
     for copy in loads:
         copy.wait()
-    for copy in halos:
+    for copy in halos[0]:
         copy.wait_recv()
 
-    row = lax.broadcasted_iota(jnp.int32, (CYCLES, CELLS_X), 0)
-    col = lax.broadcasted_iota(jnp.int32, (CYCLES, CELLS_X), 1)
-
-    @pl.loop(0, SECTOR)
-    def _(t):
-        mu = mux[t + 1]
-        half_cycle = 0.5 / (row.astype(jnp.float32) + 1.0)
-        up = half_cycle * (mu + mux[t + 2])
-        down = half_cycle * (mu + mux[t])
-        out_r = jnp.where(
-            row < CYCLES - 1, 0.5 * (mu + pltpu.roll(mu, CYCLES - 1, 0)), 0.0
-        )
-        in_r = pltpu.roll(out_r, 1, 0)
-        out_x = jnp.where(
-            col < CELLS_X - 1, 0.5 * (mu + pltpu.roll(mu, CELLS_X - 1, 1)), 0.0
-        )
-        in_x = pltpu.roll(out_x, 1, 1)
-        own = up + down + out_r + in_r + out_x + in_x
-        for f in range(FIELDS):
-            p = adjx[f, t + 1]
-            face = [1.0 - bcf[f, i].astype(jnp.float32) for i in range(3)]
-            edge = (
-                jnp.where(row == CYCLES - 1, face[2], 0.0)
-                + jnp.where(col == 0, face[0], 0.0)
-                + jnp.where(col == CELLS_X - 1, face[1], 0.0)
+    window = NEAR + 8
+    shape = (window, CELLS_X)
+    col = lax.broadcasted_iota(jnp.int32, shape, 1)
+
+    def stencil(part):
+        base = part * (CYCLES - window)
+        span = pl.ds(base, window)
+        keep = slice(8 * part, 8 * part + NEAR)
+        target = pl.ds(part * NEAR, NEAR)
+        row = lax.broadcasted_iota(jnp.int32, shape, 0) + base
+
+        @pl.loop(0, SECTOR)
+        def _(t):
+            mu = mux[t + 1, span]
+            half_cycle = 0.5 / (row[keep].astype(jnp.float32) + 1.0)
+            up = half_cycle * (mu[keep] + mux[t + 2, target])
+            down = half_cycle * (mu[keep] + mux[t, target])
+            out_r = jnp.where(
+                row < CYCLES - 1, 0.5 * (mu + pltpu.roll(mu, window - 1, 0)), 0.0
             )
-            diffused = (own + edge * mu) * p
-            diffused = diffused - up * adjx[f, t + 2] - down * adjx[f, t]
-            diffused = diffused - out_r * pltpu.roll(p, CYCLES - 1, 0)
-            diffused = diffused - in_r * pltpu.roll(p, 1, 0)
-            diffused = diffused - out_x * pltpu.roll(p, CELLS_X - 1, 1)
-            diffused = diffused - in_x * pltpu.roll(p, 1, 1)
-            total = local[f, t] + kap[f] * diffused
-            for g in range(FIELDS):
-                total = total + cpl[g, f] * adjx[g, t + 1]
-            local[f, t] = total
+            in_r = jnp.where(row > 0, pltpu.roll(out_r, 1, 0), 0.0)
+            out_x = jnp.where(
+                col < CELLS_X - 1, 0.5 * (mu + pltpu.roll(mu, CELLS_X - 1, 1)), 0.0
+            )
+            in_x = pltpu.roll(out_x, 1, 1)
+            own = up + down + (out_r + in_r + out_x + in_x)[keep]
+            for f in range(FIELDS):
+                p = adjx[f, t + 1, span]
+                face = [1.0 - bcf[i, f].astype(jnp.float32) for i in range(3)]
+                edge = (
+                    jnp.where(row[keep] == CYCLES - 1, face[2], 0.0)
+                    + jnp.where(col[keep] == 0, face[0], 0.0)
+                    + jnp.where(col[keep] == CELLS_X - 1, face[1], 0.0)
+                )
+                core = p[keep]
+                diffused = (own + edge * mu[keep]) * core
+                diffused = diffused - up * adjx[f, t + 2, target] - down * adjx[f, t, target]
+                diffused = diffused - (out_r * pltpu.roll(p, window - 1, 0))[keep]
+                diffused = diffused - (in_r * pltpu.roll(p, 1, 0))[keep]
+                diffused = diffused - out_x[keep] * pltpu.roll(core, CELLS_X - 1, 1)
+                diffused = diffused - in_x[keep] * pltpu.roll(core, 1, 1)
+                total = local[f, t, target] + kap[f] * diffused
+                for g in range(FIELDS):
+                    total = total + cpl[g, f] * adjx[g, t + 1, target]
+                local[f, t, target] = total
+
+    stencil(0)
 
     for g in range(count):
         lo, hi, _ = bounds[g]
@@ -299,20 +321,26 @@
 
         own_e[g].start()
 
-        @pl.loop(1, SECTORS)
-        def _(i):
+        for i in range(1, SECTORS):
             send_s(stage_e, recv_e, e_send, e_recv, g, SECTORS - i, sp).start()
 
-    mix(count)
+    for k in range(1, SLOTS):
+        send_a(count, k).start()
+    for copy in halos[1]:
+        copy.start()
+    for copy in halos[1]:
+        copy.wait_recv()
+    stencil(1)
 
     for g in range(count):
         lo, hi, _ = bounds[g]
+        if g == count - 1:
+            mix(count)
         own_e[g].wait()
 
-        @pl.loop(1, SECTORS)
-        def _(i):
+        for i in range(1, SECTORS):
             send_s(
-                stage_e, recv_e, e_send, e_recv, g, SECTORS - i, space_at(SECTORS - i, -1)
+                stage_e, recv_e, e_send, e_recv, g, SECTORS - i, sp
             ).wait_recv()
 
         pencils = recv_e[g][...].reshape(SECTORS, (hi - lo) * SECTOR, CELLS_X)
@@ -331,8 +359,7 @@
         )
         own_g[g].start()
 
-        @pl.loop(1, SECTORS)
-        def _(i):
+        for i in range(1, SECTORS):
             send_s(stage_g, recv_g, g_send, g_recv, g, SECTORS - i, sp).start()
 
     own_c[count].wait()
@@ -342,26 +369,17 @@
     @pl.loop(0, SECTOR)
     def _(t):
         for f in range(FIELDS):
-            outv[f, t, pl.ds(NEAR, NEAR), :] = (
+            out[0, f, t, pl.ds(NEAR, NEAR), :] = (
                 local[f, t, pl.ds(NEAR, NEAR), :] + spec[count][f, t]
             )
 
-    far = pltpu.make_async_copy(
-        outv.at[:, :, pl.ds(NEAR, NEAR), :],
-        out.at[0, :, :, pl.ds(NEAR, NEAR), :],
-        out_sem.at[count],
-    )
-    far.start()
-    writes = [far]
-
     for g in range(count):
         lo, hi, _ = bounds[g]
         own_g[g].wait()
 
-        @pl.loop(1, SECTORS)
-        def _(i):
+        for i in range(1, SECTORS):
             send_s(
-                stage_g, recv_g, g_send, g_recv, g, SECTORS - i, space_at(SECTORS - i, -1)
+                stage_g, recv_g, g_send, g_recv, g, SECTORS - i, sp
             ).wait_recv()
 
         stride = (hi - lo) * SECTOR
@@ -371,19 +389,11 @@
             for f in range(lo, hi):
                 for b in range(NEAR // 8):
                     start = b * 8 * stride + (f - lo) * SECTOR + t
-                    outv[f, t, pl.ds(b * 8, 8), :] = recv_g[g][
+                    out[0, f, t, pl.ds(b * 8, 8), :] = recv_g[g][
                         pl.ds(start, 8, stride=stride), :
                     ]
 
-        write = pltpu.make_async_copy(
-            outv.at[pl.ds(lo, hi - lo), :, pl.ds(0, NEAR), :],
-            out.at[0, pl.ds(lo, hi - lo), :, pl.ds(0, NEAR), :],
-            out_sem.at[g],
-        )
-        write.start()
-        writes.append(write)
-
-    for copy in halos:
+    for copy in halos[0] + halos[1]:
         copy.wait_send()
     for g in range(count + 1):
         for k in range(1, SLOTS):
@@ -391,13 +401,9 @@
             send_c(g, k).wait_send()
     for g in range(count):
 
-        @pl.loop(1, SECTORS)
-        def _(i):
+        for i in range(1, SECTORS):
             send_s(stage_e, recv_e, e_send, e_recv, g, SECTORS - i, sp).wait_send()
             send_s(stage_g, recv_g, g_send, g_recv, g, SECTORS - i, sp).wait_send()
-
-    for copy in writes:
-        copy.wait()
 
 
 def body(adjoint, source, viscosity, kappa, coupling, bc_flags, inst_map):
@@ -412,32 +418,39 @@
         vmem((FIELDS, SECTOR + 2, CYCLES, CELLS_X), f32),
         vmem((SECTOR + 2, CYCLES, CELLS_X), f32),
         vmem((FIELDS, SECTOR, CYCLES, CELLS_X), f32),
-        vmem((FIELDS, SECTOR, CYCLES, CELLS_X), f32),
         vmem((POINTS, POINTS), f32),
         *slabs,
         *slabs,
         *sectors,
         *(pencils * 4),
-        dma((3,)),
-        dma((4,)),
-        dma((4,)),
+        dma((8,)),
+        dma((8,)),
+        dma((8,)),
         dma((4, count + 1)),
-        dma((count + 1,)),
+        *[
+            pltpu.SMEM(x.shape, x.dtype)
+            for x in (kappa, coupling, bc_flags.T, inst_map, slot_table())
+        ],
         *[dma((count + 1, SLOTS))] * 4,
         *[dma((count, SECTORS))] * 4,
     ]
-    hbm, smem = pl.BlockSpec(memory_space=pl.ANY), pl.BlockSpec(memory_space=pltpu.SMEM)
+    hbm = pl.BlockSpec(memory_space=pltpu.HBM)
     return pl.pallas_call(
         kernel,
         out_shape=jax.ShapeDtypeStruct(adjoint.shape, f32),
-        in_specs=[hbm] * 3 + [smem] * 5,
-        out_specs=hbm,
+        in_specs=[hbm] * 8,
+        out_specs=pl.BlockSpec(memory_space=pltpu.VMEM),
         scratch_shapes=scratch,
         compiler_params=pltpu.CompilerParams(
             collective_id=0, has_side_effects=True, vmem_limit_bytes=48 * 1024 * 1024
         ),
         name="residual",
-    )(adjoint, source, viscosity, kappa, coupling, bc_flags, inst_map, slot_table())
+    )(*[
+        pltpu.with_memory_space_constraint(x, pltpu.HBM)
+        for x in (
+            adjoint, source, viscosity, kappa, coupling, bc_flags.T, inst_map, slot_table()
+        )
+    ])
 
 
 def solution(mesh):

time: 87.6 us -> 70 us (0.80); the launches traced: 86.2 us -> 69.7 us
  Pallas kernels: 78.2 us -> 68.6 us
  local copies, waits for them, and re-layouts: 8.06 us -> 1.06 us
    pallas_call x1, Pallas kernels: 78.2 us -> 68.6 us  [body(): pl.pallas_call(kernel, out_shape=jax.ShapeDtypeStruct(adjoint.shape, f32)...]
    unnamed x16 -> x1, local copies, waits for them, and re-layouts: 8.06 us -> 1.06 us
where the time goes in v2:
time: 70 us; the launch traced here: 69.7 us
  Pallas kernels  68.6 us (98%)
  local copies, waits for them, and re-layouts  1.06 us (2%)
    pallas_call x1, Pallas kernels, body(): pl.pallas_call(kernel, out_shape=jax.ShapeDtypeStruct(adjoint.shape, f32)...  68.6 us

profile of v2, /device:TPU:1, one launch (start us, length us, event | category | flops | bytes accessed | tf_op | source)
XLA Modules:
  0.0 69.7 jit_solution(6766031685064721534)
XLA Ops:
  0.0 68.6 %residual.1 = f32[1,5,8,64,128]{4,3,2,1,0:T(8,128)S(1)} custom-call(f32[1,5,8,64,128]{4,3,2,1,0:T(8,128)} %adj.1, f32[1,5,8,64,128]{4,3,2,1,0:T(8,128)} %src.1, f32[8,64,128]{2,1,0:T(8,128)} %visc.1, f32[5]{0:T(128)} %refs_0_.1, f32[5,5]{1,0:T(8,128)} %refs_1_.1, s32[3,5]{1,0:T(4,128)} %bitcast.1, s32[8]{0:T(128)} %refs_3_.1, f32[16]{0:T(128)} %constant.2.clone.refs_4_), custom_call_target="tpu_custom_call" | custom-call | tf_op jit(solution)/shard_map/residual/pallas_call | solution.py:438
  68.7 1.1 %copy.10 = f32[1,5,8,64,128]{4,3,2,1,0:T(8,128)} copy(f32[1,5,8,64,128]{4,3,2,1,0:T(8,128)S(1)} %residual.1) | data formatting | bytes 2621440

commit v3 on v2

--- a/solution.py
+++ b/solution.py
@@ -33,7 +33,7 @@
     mixed = take(count + 1)
     spec = take(count + 1)
     stage_e, recv_e, stage_g, recv_g = take(count), take(count), take(count), take(count)
-    load_sem, halo_send, halo_recv, own_sem = take(4)
+    load_sem, halo_send, halo_recv, own_sem, ready = take(5)
     held = take(5)
     kap, cpl, bcf, imap, tab = held
     a_send, a_recv, c_send, c_recv = take(4)
@@ -178,16 +178,25 @@
             barrier, inc=1, device_id={"inst": inst_at(k, 1)}, device_id_type=MESH
         )
 
-    for i in range(SECTORS - 1, 0, -1):
-        pl.semaphore_signal(
-            barrier, inc=1, device_id={"space": space_at(i, 1)}, device_id_type=MESH
-        )
+    for peer in (after, before):
+        pl.semaphore_signal(barrier, inc=1, device_id={"space": peer}, device_id_type=MESH)
+
+    def greet(j):
+        for sign in (1, -1):
+            peer = lax.rem(sp + sign * 2**j + SECTORS, SECTORS)
+            pl.semaphore_signal(
+                ready.at[j], inc=1, device_id={"space": peer}, device_id_type=MESH
+            )
+
+    def met(j):
+        pl.semaphore_wait(ready.at[j], 2)
 
     for copy in consts + loads:
         copy.start()
     for copy in own_a:
         copy.start()
-    pl.semaphore_wait(barrier, SLOTS - 1 + SECTORS - 1)
+    pl.semaphore_wait(barrier, SLOTS - 1 + 2)
+    greet(0)
 
     for g in range(count):
         for k in range(1, SLOTS):
@@ -247,8 +256,13 @@
 
     for copy in consts:
         copy.wait()
+    met(0)
+    greet(1)
     for g in range(count):
         mix(g)
+        if g == 0:
+            met(1)
+            greet(2)
 
     for copy in loads:
         copy.wait()
@@ -302,6 +316,8 @@
                 local[f, t, target] = total
 
     stencil(0)
+    met(2)
+    greet(3)
 
     for g in range(count):
         lo, hi, _ = bounds[g]
@@ -319,23 +335,20 @@
                     start = b * 8 * stride + (f - lo) * SECTOR + t
                     stage_e[g][pl.ds(start, 8, stride=stride), :] = value
 
+        if g == 0:
+            met(3)
         own_e[g].start()
 
         for i in range(1, SECTORS):
             send_s(stage_e, recv_e, e_send, e_recv, g, SECTORS - i, sp).start()
 
+    for copy in halos[1]:
+        copy.start()
     for k in range(1, SLOTS):
         send_a(count, k).start()
-    for copy in halos[1]:
-        copy.start()
-    for copy in halos[1]:
-        copy.wait_recv()
-    stencil(1)
 
     for g in range(count):
         lo, hi, _ = bounds[g]
-        if g == count - 1:
-            mix(count)
         own_e[g].wait()
 
         for i in range(1, SECTORS):
@@ -362,6 +375,10 @@
         for i in range(1, SECTORS):
             send_s(stage_g, recv_g, g_send, g_recv, g, SECTORS - i, sp).start()
 
+    mix(count)
+    for copy in halos[1]:
+        copy.wait_recv()
+    stencil(1)
     own_c[count].wait()
     for k in range(1, SLOTS):
         arrive_c(count, k).wait_recv()
@@ -427,6 +444,7 @@
         dma((8,)),
         dma((8,)),
         dma((4, count + 1)),
+        pltpu.SemaphoreType.REGULAR((4,)),
         *[
             pltpu.SMEM(x.shape, x.dtype)
             for x in (kappa, coupling, bc_flags.T, inst_map, slot_table())

time: 70 us -> 66.5 us (0.950)
  Pallas kernels: 68.6 us -> 65.3 us
    pallas_call x1, Pallas kernels: 68.6 us -> 65.3 us  [body(): pl.pallas_call(kernel, out_shape=jax.ShapeDtypeStruct(adjoint.shape, f32)...]
where the time goes in v3:
time: 66.5 us; the launch traced here: 66.4 us
  Pallas kernels  65.3 us (98%)
  local copies, waits for them, and re-layouts  1.06 us (2%)
    pallas_call x1, Pallas kernels, body(): pl.pallas_call(kernel, out_shape=jax.ShapeDtypeStruct(adjoint.shape, f32)...  65.3 us

profile of v3, /device:TPU:1, one launch (start us, length us, event | category | flops | bytes accessed | tf_op | source)
XLA Modules:
  0.0 66.4 jit_solution(8833205205322428306)
XLA Ops:
  0.0 65.3 %residual.1 = f32[1,5,8,64,128]{4,3,2,1,0:T(8,128)S(1)} custom-call(f32[1,5,8,64,128]{4,3,2,1,0:T(8,128)} %adj.1, f32[1,5,8,64,128]{4,3,2,1,0:T(8,128)} %src.1, f32[8,64,128]{2,1,0:T(8,128)} %visc.1, f32[5]{0:T(128)} %refs_0_.1, f32[5,5]{1,0:T(8,128)} %refs_1_.1, s32[3,5]{1,0:T(4,128)} %bitcast.1, s32[8]{0:T(128)} %refs_3_.1, f32[16]{0:T(128)} %constant.2.clone.refs_4_), custom_call_target="tpu_custom_call" | custom-call | tf_op jit(solution)/shard_map/residual/pallas_call | solution.py:456
  65.4 1.1 %copy.10 = f32[1,5,8,64,128]{4,3,2,1,0:T(8,128)} copy(f32[1,5,8,64,128]{4,3,2,1,0:T(8,128)S(1)} %residual.1) | data formatting | bytes 2621440

commit v4 on v3

--- a/solution.py
+++ b/solution.py
@@ -53,9 +53,9 @@
         return turn_x[(sign * (k // 2)) % 4] + flip_y[k % 2]
 
     def space_at(i, sign):
-        step = i // 4
+        step = i // 2 % 8
         kz = (step + 1) // 2 * (1 - 2 * (step % 2))
-        return turn_z[(sign * kz) % 8] + flip_s[i // 2 % 2] + flip_c[i % 2]
+        return turn_z[(sign * kz) % 8] + flip_s[i // 16] + flip_c[i % 2]
 
     loads = [
         pltpu.make_async_copy(visc, mux.at[pl.ds(1, SECTOR)], load_sem.at[0]),
@@ -199,7 +199,7 @@
     greet(0)
 
     for g in range(count):
-        for k in range(1, SLOTS):
+        for k in (5, 3, 7, 1, 4, 2, 6):
             send_a(g, k).start()
     for copy in halos[0]:
         copy.start()
@@ -250,7 +250,7 @@
                         total = total + term if j > n else total - term
                 mixed[g][n, fi, block, :] = total
 
-        for k in range(1, SLOTS):
+        for k in (5, 3, 7, 1, 4, 2, 6):
             send_c(g, k).start()
         own_c[g].start()
 
@@ -342,10 +342,10 @@
         for i in range(1, SECTORS):
             send_s(stage_e, recv_e, e_send, e_recv, g, SECTORS - i, sp).start()
 
+    for k in (5, 3, 7, 1, 4, 2, 6):
+        send_a(count, k).start()
     for copy in halos[1]:
         copy.start()
-    for k in range(1, SLOTS):
-        send_a(count, k).start()
 
     for g in range(count):
         lo, hi, _ = bounds[g]

time: 66.5 us -> 64.5 us (0.970)
  Pallas kernels: 65.3 us -> 63.4 us
    pallas_call x1, Pallas kernels: 65.3 us -> 63.4 us  [body(): pl.pallas_call(kernel, out_shape=jax.ShapeDtypeStruct(adjoint.shape, f32)...]
where the time goes in v4:
time: 64.5 us
  Pallas kernels  63.4 us (98%)
  local copies, waits for them, and re-layouts  1.06 us (2%)
    pallas_call x1, Pallas kernels, body(): pl.pallas_call(kernel, out_shape=jax.ShapeDtypeStruct(adjoint.shape, f32)...  63.4 us

profile of v4, /device:TPU:1, one launch (start us, length us, event | category | flops | bytes accessed | tf_op | source)
XLA Modules:
  0.0 64.5 jit_solution(16851202358525429829)
XLA Ops:
  0.0 63.4 %residual.1 = f32[1,5,8,64,128]{4,3,2,1,0:T(8,128)S(1)} custom-call(f32[1,5,8,64,128]{4,3,2,1,0:T(8,128)} %adj.1, f32[1,5,8,64,128]{4,3,2,1,0:T(8,128)} %src.1, f32[8,64,128]{2,1,0:T(8,128)} %visc.1, f32[5]{0:T(128)} %refs_0_.1, f32[5,5]{1,0:T(8,128)} %refs_1_.1, s32[3,5]{1,0:T(4,128)} %bitcast.1, s32[8]{0:T(128)} %refs_3_.1, f32[16]{0:T(128)} %constant.2.clone.refs_4_), custom_call_target="tpu_custom_call" | custom-call | tf_op jit(solution)/shard_map/residual/pallas_call | solution.py:456
  63.4 1.1 %copy.10 = f32[1,5,8,64,128]{4,3,2,1,0:T(8,128)} copy(f32[1,5,8,64,128]{4,3,2,1,0:T(8,128)S(1)} %residual.1) | data formatting | bytes 2621440

commit v5 on v4

--- a/solution.py
+++ b/solution.py
@@ -34,6 +34,7 @@
     spec = take(count + 1)
     stage_e, recv_e, stage_g, recv_g = take(count), take(count), take(count), take(count)
     load_sem, halo_send, halo_recv, own_sem, ready = take(5)
+    mhead, mrest = take(2)
     held = take(5)
     kap, cpl, bcf, imap, tab = held
     a_send, a_recv, c_send, c_recv = take(4)
@@ -221,6 +222,11 @@
         mtab[pl.ds(pl.multiple_of(b * 32, 32), 32), :] = weight * table + jnp.where(
             same, 1.0 - weight, 0.0
         )
+
+    whole = mtab[...]
+    mhead[...] = whole.astype(jnp.bfloat16)
+    mrest[...] = (whole - mhead[...].astype(jnp.float32)).astype(jnp.bfloat16)
+    dot = functools.partial(jnp.dot, preferred_element_type=jnp.float32)
 
     def mix(g):
         own_a[g].wait()
@@ -315,6 +321,8 @@
                     total = total + cpl[g, f] * adjx[g, t + 1, target]
                 local[f, t, target] = total
 
+    for k in (4, 2, 6):
+        send_a(count, k).start()
     stencil(0)
     met(2)
     greet(3)
@@ -342,7 +350,7 @@
         for i in range(1, SECTORS):
             send_s(stage_e, recv_e, e_send, e_recv, g, SECTORS - i, sp).start()
 
-    for k in (5, 3, 7, 1, 4, 2, 6):
+    for k in (5, 3, 7, 1):
         send_a(count, k).start()
     for copy in halos[1]:
         copy.start()
@@ -360,12 +368,9 @@
         parts = []
         for f in range(hi - lo):
             pencil = pencils[:, f * SECTOR : (f + 1) * SECTOR, :].reshape(POINTS, CELLS_X)
-            smooth = jnp.dot(
-                mtab[...],
-                pencil,
-                precision=lax.Precision.HIGHEST,
-                preferred_element_type=jnp.float32,
-            )
+            head = pencil.astype(jnp.bfloat16)
+            rest = (pencil - head.astype(jnp.float32)).astype(jnp.bfloat16)
+            smooth = dot(mhead[...], rest) + dot(mrest[...], head) + dot(mhead[...], head)
             parts.append(smooth.reshape(SECTORS, SECTOR, CELLS_X))
         stage_g[g][...] = jnp.concatenate(parts, axis=1).reshape(
             SECTORS * (hi - lo) * SECTOR, CELLS_X
@@ -445,6 +450,8 @@
         dma((8,)),
         dma((4, count + 1)),
         pltpu.SemaphoreType.REGULAR((4,)),
+        vmem((POINTS, POINTS), jnp.bfloat16),
+        vmem((POINTS, POINTS), jnp.bfloat16),
         *[
             pltpu.SMEM(x.shape, x.dtype)
             for x in (kappa, coupling, bc_flags.T, inst_map, slot_table())

time: 64.5 us -> 64.3 us (level)
  no operation moved by 1% of the time
where the time goes in v5:
time: 64.3 us; the launch traced here: 64.2 us
  Pallas kernels  63.2 us (98%)
  local copies, waits for them, and re-layouts  1.06 us (2%)
    pallas_call x1, Pallas kernels, body(): pl.pallas_call(kernel, out_shape=jax.ShapeDtypeStruct(adjoint.shape, f32)...  63.2 us

profile of v5, /device:TPU:1, one launch (start us, length us, event | category | flops | bytes accessed | tf_op | source)
XLA Modules:
  0.0 64.2 jit_solution(16152694205313286579)
XLA Ops:
  0.0 63.2 %residual.1 = f32[1,5,8,64,128]{4,3,2,1,0:T(8,128)S(1)} custom-call(f32[1,5,8,64,128]{4,3,2,1,0:T(8,128)} %adj.1, f32[1,5,8,64,128]{4,3,2,1,0:T(8,128)} %src.1, f32[8,64,128]{2,1,0:T(8,128)} %visc.1, f32[5]{0:T(128)} %refs_0_.1, f32[5,5]{1,0:T(8,128)} %refs_1_.1, s32[3,5]{1,0:T(4,128)} %bitcast.1, s32[8]{0:T(128)} %refs_3_.1, f32[16]{0:T(128)} %constant.2.clone.refs_4_), custom_call_target="tpu_custom_call" | custom-call | tf_op jit(solution)/shard_map/residual/pallas_call | solution.py:463
  63.2 1.1 %copy.10 = f32[1,5,8,64,128]{4,3,2,1,0:T(8,128)} copy(f32[1,5,8,64,128]{4,3,2,1,0:T(8,128)S(1)} %residual.1) | data formatting | bytes 2621440
